TPU v7x, 32 devices: a whole 2x2x4 slice. The times are simulated.
32 devices in a mesh: seq: 8 (over z, y), head: 4 (over x, core).
Axes of the slice: x: 2, y: 2, z: 4, core: 2. Of those that a mesh axis runs over, the one named last changes fastest.
Arguments:
- inputs: bfloat16 [2048, 2560], P('seq', 'head'), may hold values from -6 to 6
- step_sizes: float32 [40, 2048], P('head', 'seq'), may hold values from 0.1 to 1
- input_map: bfloat16 [2048, 128], P('seq'), may hold values from -1.78125 to 1.78125
- output_map: bfloat16 [2048, 128], P('seq'), may hold values from -1.78125 to 1.78125
- level_table: float32 [40, 2, 12], P('head'), may hold values from 0.25 to 2
- token_class: int32 [2048], P('seq'), may hold values from 0 to 1
- cotangent: bfloat16 [2048, 2560], P('seq', 'head'), may hold values from -6 to 6
Outputs:
- layer_out: bfloat16 [2048, 2560], P('seq', 'head')
- input_grad: bfloat16 [2048, 2560], P('seq', 'head')
- step_grad: float32 [40, 2048], P('head', 'seq')
- input_map_grad: float32 [2048, 128], P('seq')
- output_map_grad: float32 [2048, 128], P('seq')
- table_grad: float32 [40, 2, 12], P('head')
All inputs are finite; a program needn't handle non-finite values.
Results may differ from a plain program's by a relative error of at most 0.006.
Values may be sent and summed in bfloat16 or wider, within the bound.
A program may use at most 64 MiB of HBM per device.

v0:
```python
import functools
import math

import jax
import jax.numpy as jnp
from jax import lax
from jax.experimental import pallas as pl
from jax.experimental.pallas import tpu as pltpu
from jax.sharding import PartitionSpec as P

Q = 128
LANES = 128
F32 = jnp.float32
BF16 = jnp.bfloat16
HIGH = lax.Precision.HIGHEST
MESH = pl.DeviceIdType.MESH


def dot(a, b, ca, cb, precision=None):
    return lax.dot_general(
        a, b, (((ca,), (cb,)), ((), ())), precision=precision, preferred_element_type=F32
    )


def scale_of(level):
    return 1.0 if level == 0 else 2.0 ** (-(level - 1) / 2)


def kernel(
    dims,
    x_ref,
    step_ref,
    bin_ref,
    cout_ref,
    table_ref,
    class_ref,
    g_ref,
    out_ref,
    xg_ref,
    sg_ref,
    ing_ref,
    outg_ref,
    tg_ref,
    stepx,
    scaled,
    clsb,
    lev,
    scores,
    mo2,
    s0,
    q1,
    qown,
    frun,
    rrun,
    fcs,
    fsrc,
    nout,
    nback,
    score_sum,
    in_acc,
    out_acc,
    tab,
    send_f,
    recv_f,
    send_r,
    recv_r,
    part_send,
    part_recv,
    part_own,
    final,
    tsend,
    trecv,
    f_ssem,
    f_rsem,
    r_ssem,
    r_rsem,
    p_ssem,
    p_rsem,
    a_ssem,
    a_rsem,
    t_ssem,
    t_rsem,
    steprow,
    sgrow,
):
    heads, width, tokens, state, levels, nb, n_head, total = dims
    per = LANES // width
    pairs = heads // per
    sb = Q.bit_length() - 1
    mid = sb + 1
    far0 = mid + 1
    device = lax.axis_index("seq")
    mine = lax.axis_index("head")

    barrier = pltpu.get_barrier_semaphore()
    for b in range(nb):
        pl.semaphore_signal(barrier, inc=1, device_id={"seq": device ^ (1 << b)}, device_id_type=MESH)
    for i in range(1, n_head):
        pl.semaphore_signal(
            barrier, inc=1, device_id={"head": lax.rem(mine + i, n_head)}, device_id_type=MESH
        )

    lane = lax.broadcasted_iota(jnp.int32, (1, LANES), 1)
    halves = [(lane // width == j) for j in range(per)]
    half_f = [m.astype(F32) for m in halves]
    half_b = [m.astype(F32).astype(BF16) for m in halves]
    zero = jnp.zeros((state, LANES), F32)

    def wrow(p, k, level):
        row = jnp.zeros((1, LANES), F32)
        for j in range(per):
            row = jnp.where(halves[j], table_ref[p * per + j, k, level] * scale_of(level), row)
        return row

    def cols(p):
        return pl.ds(pl.multiple_of(p * LANES, LANES), LANES)

    row = class_ref[...].astype(F32)
    clsb[...] = dot(
        jnp.broadcast_to(row, (16, tokens)).astype(BF16),
        jnp.full((16, LANES), 0.0625, BF16),
        0,
        0,
    )
    t_id = lax.broadcasted_iota(jnp.int32, (Q, Q), 0)
    s_id = lax.broadcasted_iota(jnp.int32, (Q, Q), 1)
    differ = t_id ^ s_id
    level_id = jnp.zeros((Q, Q), jnp.int32)
    for bit in range(sb):
        level_id = level_id + (differ >= (1 << bit)).astype(jnp.int32)
    lev[...] = jnp.where(t_id >= s_id, level_id, -1)
    spans = [slice(c * Q, (c + 1) * Q) for c in range(2)]
    for c in range(2):
        scores[c] = dot(cout_ref[spans[c], :], bin_ref[spans[c], :], 1, 1)
        one = clsb[spans[c], :]
        mo = cout_ref[spans[c], :].astype(F32)
        mo2[c, :, :state] = (mo * (1.0 - one)).astype(BF16)
        mo2[c, :, state:] = (mo * one).astype(BF16)
    for h in range(heads):
        for c in range(2):
            steprow[h, c : c + 1, :] = step_ref[h : h + 1, spans[c]]
    score_sum[...] = jnp.zeros_like(score_sum)
    in_acc[...] = jnp.zeros_like(in_acc)
    out_acc[...] = jnp.zeros_like(out_acc)
    tab[...] = jnp.zeros_like(tab)

    def f_copy(b, p):
        return pltpu.make_async_remote_copy(
            send_f.at[b, p], recv_f.at[b, p], f_ssem.at[b, p], f_rsem.at[b, p],
            device_id={"seq": device ^ (1 << b)}, device_id_type=MESH,
        )

    def r_copy(b, k, p):
        return pltpu.make_async_remote_copy(
            send_r.at[b, k, p], recv_r.at[b, k, p], r_ssem.at[b, k, p], r_rsem.at[b, k, p],
            device_id={"seq": device ^ (1 << b)}, device_id_type=MESH,
        )

    bit_of = [(device >> b) & 1 for b in range(nb)]
    above = [device >> (b + 1) for b in range(nb)]
    ones = [(1 << (nb - b - 1)) - 1 for b in range(nb)]
    f_sent = [(bit_of[b] == 0) | (above[b] != ones[b]) for b in range(nb)]
    f_came = [(bit_of[b] == 1) | (above[b] != ones[b]) for b in range(nb)]
    c_sent = [(bit_of[b] == 1) & (above[b] == 0) for b in range(nb)]
    c_came = [(bit_of[b] == 0) & (above[b] == 0) for b in range(nb)]
    r_both = [above[b] != 0 for b in range(nb)]

    def start(b, p):
        @pl.when(f_sent[b])
        def _():
            send_f[b, p] = frun[p].astype(BF16)
            f_copy(b, p).start()

        @pl.when(c_sent[b])
        def _():
            send_r[b, 0, p] = (
                wrow(p, 0, far0 + b) * rrun[0, p] + wrow(p, 1, far0 + b) * rrun[1, p]
            ).astype(BF16)
            r_copy(b, 0, p).start()

        @pl.when(r_both[b])
        def _():
            for k in range(2):
                send_r[b, k, p] = rrun[k, p].astype(BF16)
                r_copy(b, k, p).start()

    def put_rows(k, level, p, value):
        for j in range(per):
            tab[k * levels + level, pl.ds(p * per + j, 1), :] = value * half_f[j]

    def combine(b, p):
        @pl.when(f_came[b])
        def _():
            f_copy(b, p).wait_recv()
            got = recv_f[b, p].astype(F32)
            frun[p] = frun[p] + got

        @pl.when(bit_of[b] == 1)
        def _():
            got = recv_f[b, p].astype(F32)
            for k in range(2):
                fcs[k, p] = fcs[k, p] + wrow(p, k, far0 + b) * got
                put_rows(k, far0 + b, p, jnp.sum(got * qown[k, p], axis=0, keepdims=True))

        @pl.when(c_came[b])
        def _():
            r_copy(b, 0, p).wait_recv()
            fsrc[p] = fsrc[p] + recv_r[b, 0, p].astype(F32)

        @pl.when(r_both[b])
        def _():
            for k in range(2):
                r_copy(b, k, p).wait_recv()
                got = recv_r[b, k, p].astype(F32)
                rrun[k, p] = rrun[k, p] + got

            @pl.when(bit_of[b] == 0)
            def _():
                fsrc[p] = (
                    fsrc[p]
                    + wrow(p, 0, far0 + b) * recv_r[b, 0, p].astype(F32)
                    + wrow(p, 1, far0 + b) * recv_r[b, 1, p].astype(F32)
                )

    def states(p, carry):
        picks = (
            lax.broadcasted_iota(jnp.int32, (heads, LANES), 0)
            == p * per + lax.broadcasted_iota(jnp.int32, (heads, LANES), 1) // width
        ).astype(F32)
        grown = dot(step_ref[...], picks, 0, 0, HIGH)
        stepx[p] = grown
        sc = (x_ref[:, cols(p)].astype(F32) * grown).astype(BF16)
        scaled[p] = sc
        st = [dot(bin_ref[spans[c], :], sc[spans[c]], 0, 0) for c in range(2)]
        s0[p] = st[0]
        frun[p] = st[0] + st[1]
        q = [dot(mo2[c], g_ref[spans[c], cols(p)], 0, 0) for c in range(2)]
        for k in range(2):
            part = [q[c][k * state : (k + 1) * state] for c in range(2)]
            q1[k, p] = part[1]
            both = part[0] + part[1]
            qown[k, p] = both
            rrun[k, p] = both
            fcs[k, p] = zero
            put_rows(k, mid, p, jnp.sum(st[0] * part[1], axis=0, keepdims=True))
        fsrc[p] = zero
        return carry

    def begin(p, carry):
        start(0, p)
        return carry

    def states_begin(p, carry):
        states(p, carry)
        return begin(p, carry)

    pl.semaphore_wait(barrier, nb + n_head - 1)
    lax.fori_loop(0, pairs, states_begin, 0)

    def near(p, carry):
        lv = lev[...]
        hit = [lv == level for level in range(sb + 1)]
        weights = []
        for j in range(per):
            rows = []
            for k in range(2):
                acc = jnp.zeros((Q, Q), F32)
                for level in range(sb + 1):
                    acc = jnp.where(
                        hit[level], table_ref[p * per + j, k, level] * scale_of(level), acc
                    )
                rows.append(acc)
            weights.append(rows)
        terms = [[jnp.zeros((Q, Q), F32) for k in range(2)] for j in range(per)]
        for c in range(2):
            x = x_ref[spans[c], cols(p)]
            g = g_ref[spans[c], cols(p)]
            xs = jnp.concatenate([x * half_b[j] for j in range(per)], axis=0)
            gs = jnp.concatenate([g * half_b[j] for j in range(per)], axis=0)
            mg = dot(gs, x, 1, 1)
            is_one = clsb[spans[c], :] > 0.5
            score = scores[c]
            mixes = []
            total_sg = score_sum[c]
            for j in range(per):
                head = p * per + j
                step = steprow[head, c : c + 1, :]
                weight = jnp.where(is_one, weights[j][1], weights[j][0])
                ws = weight * step
                mgj = mg[j * Q : (j + 1) * Q]
                mixes.append((score * ws).astype(BF16))
                total_sg = total_sg + mgj * ws
                graded = mgj * score
                sgrow[head, c : c + 1, :] = jnp.sum(graded * weight, axis=0, keepdims=True)
                term = graded * step
                terms[j][0] = terms[j][0] + jnp.where(is_one, 0.0, term)
                terms[j][1] = terms[j][1] + jnp.where(is_one, term, 0.0)
            score_sum[c] = total_sg
            nout[p, spans[c], :] = dot(jnp.concatenate(mixes, axis=1), xs, 1, 0)
            nback[p, spans[c], :] = dot(jnp.concatenate(mixes, axis=0), gs, 0, 0)
        for j in range(per):
            for k in range(2):
                term = terms[j][k]
                for level in range(sb + 1):
                    if level <= 3:
                        value = jnp.sum(jnp.where(hit[level], term, 0.0), axis=0, keepdims=True)
                    else:
                        size = 1 << (level - 1)
                        value = jnp.zeros((1, LANES), F32)
                        for odd in range(1, Q // size, 2):
                            rows = jnp.sum(term[odd * size : (odd + 1) * size], axis=0, keepdims=True)
                            value = jnp.where(lane // size == odd - 1, rows, value)
                    tab[k * levels + level, pl.ds(p * per + j, 1), :] = value
        return carry

    def near_combine(p, carry):
        near(p, carry)
        combine(0, p)
        if nb > 1:
            start(1, p)
        return carry

    lax.fori_loop(0, pairs, near_combine, 0)

    for b in range(1, nb):
        def step_b(p, carry, b=b):
            combine(b, p)
            if b + 1 < nb:
                start(b + 1, p)
            return carry

        lax.fori_loop(0, pairs, step_b, 0)

    def table_copy(b):
        return pltpu.make_async_remote_copy(
            tsend.at[b], trecv.at[b], t_ssem.at[b], t_rsem.at[b],
            device_id={"seq": device ^ (1 << b)}, device_id_type=MESH,
        )

    table_sum = []
    for k in range(2):
        acc = jnp.zeros((heads, LANES), F32)
        for level in range(levels):
            col = jnp.sum(tab[k * levels + level], axis=1, keepdims=True)
            acc = jnp.where(lane == level, col * (scale_of(level) / math.sqrt(total)), acc)
        table_sum.append(acc)
    for k in range(2):
        tsend[0, k, :heads, :] = table_sum[k]
    table_copy(0).start()

    def far(p, carry):
        for c in range(2):
            cs = []
            for k in range(2):
                value = fcs[k, p]
                if c == 1:
                    value = value + wrow(p, k, mid) * s0[p]
                cs.append(value.astype(BF16))
            cs = jnp.concatenate(cs, axis=0)
            src = fsrc[p]
            if c == 0:
                src = src + wrow(p, 0, mid) * q1[0, p] + wrow(p, 1, mid) * q1[1, p]
            src = src.astype(BF16)
            read = dot(mo2[c], cs, 1, 0)
            out_ref[spans[c], cols(p)] = (nout[p, spans[c], :] + read).astype(BF16)
            vg = dot(bin_ref[spans[c], :], src, 1, 0)
            xg_ref[spans[c], cols(p)] = (
                nback[p, spans[c], :] + stepx[p, spans[c], :] * vg
            ).astype(BF16)
            picks = jnp.concatenate(half_f + [jnp.zeros((8 - per, LANES), F32)], axis=0)
            far_step = dot(picks, x_ref[spans[c], cols(p)].astype(F32) * vg, 1, 1, HIGH)
            for j in range(per):
                at = (p * per + j, slice(c, c + 1), slice(None))
                sgrow[at] = sgrow[at] + far_step[j : j + 1]
            in_acc[c] = in_acc[c] + dot(scaled[p, spans[c], :], src, 1, 1)
            out_acc[c] = out_acc[c] + dot(g_ref[spans[c], cols(p)], cs, 1, 1)
        return carry

    lax.fori_loop(0, pairs, far, 0)

    for h in range(heads):
        for c in range(2):
            sg_ref[h : h + 1, spans[c]] = sgrow[h, c : c + 1, :]

    grads = [[], []]
    for c in range(2):
        sgb = score_sum[c].astype(BF16)
        is_one = clsb[spans[c], :] > 0.5
        acc = out_acc[c]
        grads[0].append(in_acc[c] + dot(sgb, cout_ref[spans[c], :], 0, 0))
        grads[1].append(
            jnp.where(is_one, acc[:, state:], acc[:, :state])
            + dot(sgb, bin_ref[spans[c], :], 1, 0)
        )
    full = jnp.concatenate(grads[0] + grads[1], axis=0)
    rows = 2 * tokens // n_head
    for q in range(n_head):
        part_own[q] = full[q * rows : (q + 1) * rows]
        part_send[q] = full[q * rows : (q + 1) * rows].astype(BF16)

    def part_copy(i):
        to = lax.rem(mine + i, n_head)
        return pltpu.make_async_remote_copy(
            part_send.at[to], part_recv.at[i], p_ssem.at[i], p_rsem.at[i],
            device_id={"head": to}, device_id_type=MESH,
        )

    def all_copy(i, slot):
        to = lax.rem(mine + i, n_head)
        return pltpu.make_async_remote_copy(
            final.at[slot], final.at[slot], a_ssem.at[i], a_rsem.at[i],
            device_id={"head": to}, device_id_type=MESH,
        )

    for i in range(1, n_head):
        part_copy(i).start()
    for b in range(nb):
        table_copy(b).wait_recv()
        for k in range(2):
            table_sum[k] = table_sum[k] + trecv[b, k, :heads, :]
        if b + 1 < nb:
            for k in range(2):
                tsend[b + 1, k, :heads, :] = table_sum[k]
            table_copy(b + 1).start()
        if b == 0:
            summed = part_own[mine]
            for i in range(1, n_head):
                part_copy(i).wait_recv()
                summed = summed + part_recv[i].astype(F32)
            final[mine] = summed.astype(BF16)
            for i in range(1, n_head):
                all_copy(i, mine).start()
    for k in range(2):
        tg_ref[:, k, :] = table_sum[k][:, :levels]
    for i in range(1, n_head):
        all_copy(i, lax.rem(mine + n_head - i, n_head)).wait_recv()
    per_out = n_head // 2
    for q in range(n_head):
        where = (slice((q % per_out) * rows, (q % per_out + 1) * rows), slice(None))
        (ing_ref if q < per_out else outg_ref)[where] = final[q].astype(F32)

    for i in range(1, n_head):
        part_copy(i).wait_send()
        all_copy(i, mine).wait_send()
    for b in range(nb):
        table_copy(b).wait_send()

        def drain(p, carry, b=b):
            @pl.when(f_sent[b])
            def _():
                f_copy(b, p).wait_send()

            @pl.when(c_sent[b])
            def _():
                r_copy(b, 0, p).wait_send()

            @pl.when(r_both[b])
            def _():
                for k in range(2):
                    r_copy(b, k, p).wait_send()

            return carry

        lax.fori_loop(0, pairs, drain, 0)


def local(inputs, step_sizes, input_map, output_map, level_table, token_class, cotangent):
    tokens, state = input_map.shape
    heads = step_sizes.shape[0]
    width = inputs.shape[1] // heads
    levels = level_table.shape[2]
    n_seq = lax.axis_size("seq")
    n_head = lax.axis_size("head")
    nb = n_seq.bit_length() - 1
    per = LANES // width
    pairs = heads // per
    assert tokens == 2 * Q and heads % per == 0 and n_head % 2 == 0 and nb > 0
    assert level_table.shape[1] == 2 and state == Q
    dims = (heads, width, tokens, state, levels, nb, n_head, float(tokens * n_seq))
    rows = 2 * tokens // n_head
    vmem = pl.BlockSpec(memory_space=pltpu.VMEM)
    smem = pl.BlockSpec(memory_space=pltpu.SMEM)
    dma = pltpu.SemaphoreType.DMA
    unit = (pairs, state, LANES)
    tall = (pairs, tokens, LANES)
    padded = -(-heads // 8) * 8
    return pl.pallas_call(
        functools.partial(kernel, dims),
        out_shape=(
            jax.ShapeDtypeStruct(inputs.shape, BF16),
            jax.ShapeDtypeStruct(inputs.shape, BF16),
            jax.ShapeDtypeStruct(step_sizes.shape, F32),
            jax.ShapeDtypeStruct(input_map.shape, F32),
            jax.ShapeDtypeStruct(output_map.shape, F32),
            jax.ShapeDtypeStruct(level_table.shape, F32),
        ),
        in_specs=[vmem, vmem, vmem, vmem, smem, vmem, vmem],
        out_specs=(vmem,) * 6,
        scratch_shapes=[
            pltpu.VMEM(tall, F32),
            pltpu.VMEM(tall, BF16),
            pltpu.VMEM((tokens, LANES), F32),
            pltpu.VMEM((Q, Q), jnp.int32),
            pltpu.VMEM((2, Q, Q), F32),
            pltpu.VMEM((2, Q, 2 * state), BF16),
            pltpu.VMEM(unit, F32),
            pltpu.VMEM((2, *unit), F32),
            pltpu.VMEM((2, *unit), F32),
            pltpu.VMEM(unit, F32),
            pltpu.VMEM((2, *unit), F32),
            pltpu.VMEM((2, *unit), F32),
            pltpu.VMEM(unit, F32),
            pltpu.VMEM(tall, F32),
            pltpu.VMEM(tall, F32),
            pltpu.VMEM((2, Q, Q), F32),
            pltpu.VMEM((2, Q, state), F32),
            pltpu.VMEM((2, Q, 2 * state), F32),
            pltpu.VMEM((2 * levels, heads, LANES), F32),
            pltpu.VMEM((nb, *unit), BF16),
            pltpu.VMEM((nb, *unit), BF16),
            pltpu.VMEM((nb, 2, *unit), BF16),
            pltpu.VMEM((nb, 2, *unit), BF16),
            pltpu.VMEM((n_head, rows, state), BF16),
            pltpu.VMEM((n_head, rows, state), BF16),
            pltpu.VMEM((n_head, rows, state), F32),
            pltpu.VMEM((n_head, rows, state), BF16),
            pltpu.VMEM((nb, 2, padded, LANES), F32),
            pltpu.VMEM((nb, 2, padded, LANES), F32),
            dma((nb, pairs)),
            dma((nb, pairs)),
            dma((nb, 2, pairs)),
            dma((nb, 2, pairs)),
            dma((n_head,)),
            dma((n_head,)),
            dma((n_head,)),
            dma((n_head,)),
            dma((nb,)),
            dma((nb,)),
            pltpu.VMEM((heads, 2, LANES), F32),
            pltpu.VMEM((heads, 2, LANES), F32),
        ],
        compiler_params=pltpu.CompilerParams(
            collective_id=0, has_side_effects=True, vmem_limit_bytes=48 << 20
        ),
    )(
        inputs, step_sizes, input_map, output_map, level_table,
        token_class.reshape(1, tokens), cotangent,
    )


def solution(mesh):
    placed = (
        P("seq", "head"),
        P("head", "seq"),
        P("seq", None),
        P("seq", None),
        P("head", None, None),
        P("seq"),
        P("seq", "head"),
    )
    return jax.shard_map(
        local,
        mesh=mesh,
        in_specs=placed,
        out_specs=(
            P("seq", "head"),
            P("seq", "head"),
            P("head", "seq"),
            P("seq", None),
            P("seq", None),
            P("head", None, None),
        ),
        check_vma=False,
    )
```

profile of v0, /device:TPU:0, one launch (start us, length us, event | category | flops | bytes accessed | tf_op | source)
XLA Modules:
  0.0 48.7 jit_solution(4799908880152495589)
XLA Ops:
  0.6 0.0 copy-start.6
  0.6 0.7 %copy-done.6 = s32[256]{0:T(256)S(1)} copy-done((s32[256]{0:T(256)S(1)}, s32[256]{0:T(256)}, u32[]{:S(2)}) %copy-start.6) | copy-done | bytes 1048
  1.3 0.0 copy-start
  1.3 1.0 %copy-done = bf16[256,640]{1,0:T(8,128)(2,1)S(1)} copy-done((bf16[256,640]{1,0:T(8,128)(2,1)S(1)}, bf16[256,640]{1,0:T(8,128)(2,1)}, u32[]{:S(2)}) %copy-start) | copy-done | bytes 327704
  2.3 0.0 copy-start.1
  2.3 1.0 %copy-done.1 = bf16[256,640]{1,0:T(8,128)(2,1)S(1)} copy-done((bf16[256,640]{1,0:T(8,128)(2,1)S(1)}, bf16[256,640]{1,0:T(8,128)(2,1)}, u32[]{:S(2)}) %copy-start.1) | copy-done | bytes 327704
  3.3 0.0 copy-start.2
  3.3 0.8 %copy-done.2 = bf16[256,128]{1,0:T(8,128)(2,1)S(1)} copy-done((bf16[256,128]{1,0:T(8,128)(2,1)S(1)}, bf16[256,128]{1,0:T(8,128)(2,1)}, u32[]{:S(2)}) %copy-start.2) | copy-done | bytes 65560
  4.1 0.0 copy-start.3
  4.1 0.8 %copy-done.3 = bf16[256,128]{1,0:T(8,128)(2,1)S(1)} copy-done((bf16[256,128]{1,0:T(8,128)(2,1)S(1)}, bf16[256,128]{1,0:T(8,128)(2,1)}, u32[]{:S(2)}) %copy-start.3) | copy-done | bytes 65560
  4.9 0.0 copy-start.4
  4.9 0.7 %copy-done.4 = f32[10,256]{1,0:T(8,128)S(1)} copy-done((f32[10,256]{1,0:T(8,128)S(1)}, f32[10,256]{1,0:T(8,128)}, u32[]{:S(2)}) %copy-start.4) | copy-done | bytes 10264
  5.7 0.0 copy-start.5
  5.7 0.7 %copy-done.5 = f32[10,2,12]{2,1,0:T(2,128)S(1)} copy-done((f32[10,2,12]{2,1,0:T(2,128)S(1)}, f32[10,2,12]{2,1,0:T(2,128)}, u32[]{:S(2)}) %copy-start.5) | copy-done | bytes 984
  6.4 38.4 %shard_map.118 = (bf16[256,640]{1,0:T(8,128)(2,1)S(1)}, bf16[256,640]{1,0:T(8,128)(2,1)S(1)}, f32[10,256]{1,0:T(8,128)S(1)}, f32[256,128]{1,0:T(8,128)S(1)}, f32...) custom-call(bf16[256,640]{1,0:T(8,128)(2,1)S(1)} %copy-done, f32[10,256]{1,0:T(8,128)S(1)} %copy-done.4, ...), custom_call_target="tpu_custom_call" | custom-call | tf_op jit(solution)/shard_map/pallas_call | solution.py:487
  44.8 0.7 %copy.19 = bf16[256,640]{1,0:T(8,128)(2,1)} copy(bf16[256,640]{1,0:T(8,128)(2,1)S(1)} %get-tuple-element.12) | data formatting | bytes 655360
  45.5 0.7 %copy.20 = bf16[256,640]{1,0:T(8,128)(2,1)} copy(bf16[256,640]{1,0:T(8,128)(2,1)S(1)} %get-tuple-element.13) | data formatting | bytes 655360
  46.2 0.6 %copy.21 = f32[10,256]{1,0:T(8,128)} copy(f32[10,256]{1,0:T(8,128)S(1)} %get-tuple-element.14) | data formatting | bytes 20480
  46.8 0.7 %copy.22 = f32[256,128]{1,0:T(8,128)} copy(f32[256,128]{1,0:T(8,128)S(1)} %get-tuple-element.15) | data formatting | bytes 262144
  47.5 0.7 %copy.23 = f32[256,128]{1,0:T(8,128)} copy(f32[256,128]{1,0:T(8,128)S(1)} %get-tuple-element.16) | data formatting | bytes 262144
  48.1 0.6 %copy.24 = f32[10,2,12]{2,1,0:T(2,128)} copy(f32[10,2,12]{2,1,0:T(2,128)S(1)} %get-tuple-element.17) | data formatting | bytes 1920
Async XLA Ops:
  0.6 0.7 %copy-start.6 = (s32[256]{0:T(256)S(1)}, s32[256]{0:T(256)}, u32[]{:S(2)}) copy-start(s32[256]{0:T(256)} %param.12) | copy-start | bytes 3076
  1.3 1.0 %copy-start = (bf16[256,640]{1,0:T(8,128)(2,1)S(1)}, bf16[256,640]{1,0:T(8,128)(2,1)}, u32[]{:S(2)}) copy-start(bf16[256,640]{1,0:T(8,128)(2,1)} %x_ref.1) | copy-start | bytes 983044
  2.3 1.0 %copy-start.1 = (bf16[256,640]{1,0:T(8,128)(2,1)S(1)}, bf16[256,640]{1,0:T(8,128)(2,1)}, u32[]{:S(2)}) copy-start(bf16[256,640]{1,0:T(8,128)(2,1)} %g_ref.1) | copy-start | bytes 983044
  3.3 0.8 %copy-start.2 = (bf16[256,128]{1,0:T(8,128)(2,1)S(1)}, bf16[256,128]{1,0:T(8,128)(2,1)}, u32[]{:S(2)}) copy-start(bf16[256,128]{1,0:T(8,128)(2,1)} %bin_ref.1) | copy-start | bytes 196612
  4.1 0.8 %copy-start.3 = (bf16[256,128]{1,0:T(8,128)(2,1)S(1)}, bf16[256,128]{1,0:T(8,128)(2,1)}, u32[]{:S(2)}) copy-start(bf16[256,128]{1,0:T(8,128)(2,1)} %cout_ref.1) | copy-start | bytes 196612
  4.9 0.7 %copy-start.4 = (f32[10,256]{1,0:T(8,128)S(1)}, f32[10,256]{1,0:T(8,128)}, u32[]{:S(2)}) copy-start(f32[10,256]{1,0:T(8,128)} %step_ref.1) | copy-start | bytes 30724
  5.7 0.7 %copy-start.5 = (f32[10,2,12]{2,1,0:T(2,128)S(1)}, f32[10,2,12]{2,1,0:T(2,128)}, u32[]{:S(2)}) copy-start(f32[10,2,12]{2,1,0:T(2,128)} %table_ref.1) | copy-start | bytes 2884
where the time goes:
time: 49.1 us; the launch traced here: 48.7 us
  Pallas kernels  38.4 us (78%)
  local copies, waits for them, and re-layouts  9.68 us (20%)
  between operations  0.66 us (1%)
    pallas_call x1, Pallas kernels, local(): pl.pallas_call(functools.partial(kernel, dims), out_shape=(jax.ShapeDtype...  38.4 us
    unnamed x20, local copies, waits for them, and re-layouts  9.68 us

commit v1 on v0

--- a/solution.py
+++ b/solution.py
@@ -28,13 +28,13 @@
 
 def kernel(
     dims,
-    x_ref,
-    step_ref,
-    bin_ref,
-    cout_ref,
+    x_hbm,
+    step_hbm,
+    bin_hbm,
+    cout_hbm,
     table_ref,
-    class_ref,
-    g_ref,
+    class_hbm,
+    g_hbm,
     out_ref,
     xg_ref,
     sg_ref,
@@ -82,6 +82,15 @@
     t_rsem,
     steprow,
     sgrow,
+    class_b,
+    source_b,
+    x_ref,
+    step_ref,
+    bin_ref,
+    cout_ref,
+    class_ref,
+    g_ref,
+    in_sem,
 ):
     heads, width, tokens, state, levels, nb, n_head, total = dims
     per = LANES // width
@@ -100,6 +109,22 @@
             barrier, inc=1, device_id={"head": lax.rem(mine + i, n_head)}, device_id_type=MESH
         )
 
+    loads = [
+        pltpu.make_async_copy(src, dst, in_sem.at[i])
+        for i, (src, dst) in enumerate(
+            [
+                (class_hbm, class_ref),
+                (cout_hbm, cout_ref),
+                (bin_hbm, bin_ref),
+                (step_hbm, step_ref),
+                (x_hbm, x_ref),
+                (g_hbm, g_ref),
+            ]
+        )
+    ]
+    for load in loads:
+        load.start()
+
     lane = lax.broadcasted_iota(jnp.int32, (1, LANES), 1)
     halves = [(lane // width == j) for j in range(per)]
     half_f = [m.astype(F32) for m in halves]
@@ -115,6 +140,8 @@
     def cols(p):
         return pl.ds(pl.multiple_of(p * LANES, LANES), LANES)
 
+    for load in loads:
+        load.wait()
     row = class_ref[...].astype(F32)
     clsb[...] = dot(
         jnp.broadcast_to(row, (16, tokens)).astype(BF16),
@@ -161,9 +188,15 @@
     ones = [(1 << (nb - b - 1)) - 1 for b in range(nb)]
     f_sent = [(bit_of[b] == 0) | (above[b] != ones[b]) for b in range(nb)]
     f_came = [(bit_of[b] == 1) | (above[b] != ones[b]) for b in range(nb)]
-    c_sent = [(bit_of[b] == 1) & (above[b] == 0) for b in range(nb)]
-    c_came = [(bit_of[b] == 0) & (above[b] == 0) for b in range(nb)]
-    r_both = [above[b] != 0 for b in range(nb)]
+    count = [sum(bit_of[b + 1 :], jnp.int32(0)) for b in range(nb)]
+    c_sent = [(bit_of[b] == 1) & (count[b] <= 1) for b in range(nb)]
+    c_came = [(bit_of[b] == 0) & (count[b] <= 1) for b in range(nb)]
+    r_none = [count[b] == 0 for b in range(nb)]
+    r_one = [count[b] == 1 for b in range(nb)]
+    r_both = [count[b] >= 2 for b in range(nb)]
+
+    def combined(p, level_row):
+        return level_row(0) * rrun[0, p] + level_row(1) * rrun[1, p]
 
     def start(b, p):
         @pl.when(f_sent[b])
@@ -173,10 +206,41 @@
 
         @pl.when(c_sent[b])
         def _():
-            send_r[b, 0, p] = (
-                wrow(p, 0, far0 + b) * rrun[0, p] + wrow(p, 1, far0 + b) * rrun[1, p]
-            ).astype(BF16)
+            def now():
+                return combined(p, lambda k: wrow(p, k, far0 + b)).astype(BF16)
+
+            if b == 0:
+                send_r[b, 0, p] = now()
+            else:
+
+                @pl.when(r_one[b])
+                def _():
+                    send_r[b, 0, p] = now()
+
+                @pl.when(r_none[b])
+                def _():
+                    send_r[b, 0, p] = rrun[0, p].astype(BF16)
+
             r_copy(b, 0, p).start()
+
+        @pl.when(r_one[b])
+        def _():
+            def later(k):
+                row = wrow(p, k, far0 + nb - 1)
+                for other in range(b + 1, nb - 1):
+                    row = jnp.where(bit_of[other] == 1, wrow(p, k, far0 + other), row)
+                return row
+
+            if b == 0:
+                rrun[0, p] = combined(p, later)
+            else:
+
+                @pl.when(bit_of[b] == 1)
+                def _():
+                    rrun[0, p] = combined(p, later)
+
+            send_r[b, 1, p] = rrun[0, p].astype(BF16)
+            r_copy(b, 1, p).start()
 
         @pl.when(r_both[b])
         def _():
@@ -206,6 +270,11 @@
         def _():
             r_copy(b, 0, p).wait_recv()
             fsrc[p] = fsrc[p] + recv_r[b, 0, p].astype(F32)
+
+        @pl.when(r_one[b])
+        def _():
+            r_copy(b, 1, p).wait_recv()
+            rrun[0, p] = rrun[0, p] + recv_r[b, 1, p].astype(F32)
 
         @pl.when(r_both[b])
         def _():
@@ -313,42 +382,7 @@
                     tab[k * levels + level, pl.ds(p * per + j, 1), :] = value
         return carry
 
-    def near_combine(p, carry):
-        near(p, carry)
-        combine(0, p)
-        if nb > 1:
-            start(1, p)
-        return carry
-
-    lax.fori_loop(0, pairs, near_combine, 0)
-
-    for b in range(1, nb):
-        def step_b(p, carry, b=b):
-            combine(b, p)
-            if b + 1 < nb:
-                start(b + 1, p)
-            return carry
-
-        lax.fori_loop(0, pairs, step_b, 0)
-
-    def table_copy(b):
-        return pltpu.make_async_remote_copy(
-            tsend.at[b], trecv.at[b], t_ssem.at[b], t_rsem.at[b],
-            device_id={"seq": device ^ (1 << b)}, device_id_type=MESH,
-        )
-
-    table_sum = []
-    for k in range(2):
-        acc = jnp.zeros((heads, LANES), F32)
-        for level in range(levels):
-            col = jnp.sum(tab[k * levels + level], axis=1, keepdims=True)
-            acc = jnp.where(lane == level, col * (scale_of(level) / math.sqrt(total)), acc)
-        table_sum.append(acc)
-    for k in range(2):
-        tsend[0, k, :heads, :] = table_sum[k]
-    table_copy(0).start()
-
-    def far(p, carry):
+    def far_maps(p):
         for c in range(2):
             cs = []
             for k in range(2):
@@ -361,6 +395,15 @@
             if c == 0:
                 src = src + wrow(p, 0, mid) * q1[0, p] + wrow(p, 1, mid) * q1[1, p]
             src = src.astype(BF16)
+            class_b[c, p] = cs
+            source_b[c, p] = src
+            in_acc[c] = in_acc[c] + dot(scaled[p, spans[c], :], src, 1, 1)
+            out_acc[c] = out_acc[c] + dot(g_ref[spans[c], cols(p)], cs, 1, 1)
+
+    def far_values(p):
+        for c in range(2):
+            cs = class_b[c, p]
+            src = source_b[c, p]
             read = dot(mo2[c], cs, 1, 0)
             out_ref[spans[c], cols(p)] = (nout[p, spans[c], :] + read).astype(BF16)
             vg = dot(bin_ref[spans[c], :], src, 1, 0)
@@ -372,15 +415,34 @@
             for j in range(per):
                 at = (p * per + j, slice(c, c + 1), slice(None))
                 sgrow[at] = sgrow[at] + far_step[j : j + 1]
-            in_acc[c] = in_acc[c] + dot(scaled[p, spans[c], :], src, 1, 1)
-            out_acc[c] = out_acc[c] + dot(g_ref[spans[c], cols(p)], cs, 1, 1)
+
+    lag = 2
+
+    def pipeline(i, carry):
+        last = i - lag * (nb - 1)
+
+        @pl.when(last > 0)
+        def _():
+            far_values(last - 1)
+
+        @pl.when(i < pairs)
+        def _():
+            near(i, 0)
+
+        for b in range(nb):
+            p = i - lag * b
+
+            @pl.when((p >= 0) & (p < pairs))
+            def _(b=b, p=p):
+                combine(b, p)
+                if b + 1 < nb:
+                    start(b + 1, p)
+                else:
+                    far_maps(p)
+
         return carry
 
-    lax.fori_loop(0, pairs, far, 0)
-
-    for h in range(heads):
-        for c in range(2):
-            sg_ref[h : h + 1, spans[c]] = sgrow[h, c : c + 1, :]
+    lax.fori_loop(0, pairs + lag * (nb - 1), pipeline, 0)
 
     grads = [[], []]
     for c in range(2):
@@ -414,6 +476,27 @@
 
     for i in range(1, n_head):
         part_copy(i).start()
+    def table_copy(b):
+        return pltpu.make_async_remote_copy(
+            tsend.at[b], trecv.at[b], t_ssem.at[b], t_rsem.at[b],
+            device_id={"seq": device ^ (1 << b)}, device_id_type=MESH,
+        )
+
+    table_sum = []
+    for k in range(2):
+        acc = jnp.zeros((heads, LANES), F32)
+        for level in range(levels):
+            col = jnp.sum(tab[k * levels + level], axis=1, keepdims=True)
+            acc = jnp.where(lane == level, col * (scale_of(level) / math.sqrt(total)), acc)
+        table_sum.append(acc)
+    for k in range(2):
+        tsend[0, k, :heads, :] = table_sum[k]
+    table_copy(0).start()
+
+    far_values(pairs - 1)
+    for h in range(heads):
+        for c in range(2):
+            sg_ref[h : h + 1, spans[c]] = sgrow[h, c : c + 1, :]
     for b in range(nb):
         table_copy(b).wait_recv()
         for k in range(2):
@@ -454,6 +537,10 @@
             def _():
                 r_copy(b, 0, p).wait_send()
 
+            @pl.when(r_one[b])
+            def _():
+                r_copy(b, 1, p).wait_send()
+
             @pl.when(r_both[b])
             def _():
                 for k in range(2):
@@ -462,6 +549,15 @@
             return carry
 
         lax.fori_loop(0, pairs, drain, 0)
+
+
+def write_out(*refs):
+    sem = refs[-1]
+    copies = [pltpu.make_async_copy(refs[i], refs[6 + i], sem.at[i]) for i in range(6)]
+    for copy in copies:
+        copy.start()
+    for copy in copies:
+        copy.wait()
 
 
 def local(inputs, step_sizes, input_map, output_map, level_table, token_class, cotangent):
@@ -479,12 +575,13 @@
     dims = (heads, width, tokens, state, levels, nb, n_head, float(tokens * n_seq))
     rows = 2 * tokens // n_head
     vmem = pl.BlockSpec(memory_space=pltpu.VMEM)
+    hbm = pl.BlockSpec(memory_space=pltpu.HBM)
     smem = pl.BlockSpec(memory_space=pltpu.SMEM)
     dma = pltpu.SemaphoreType.DMA
     unit = (pairs, state, LANES)
     tall = (pairs, tokens, LANES)
     padded = -(-heads // 8) * 8
-    return pl.pallas_call(
+    results = pl.pallas_call(
         functools.partial(kernel, dims),
         out_shape=(
             jax.ShapeDtypeStruct(inputs.shape, BF16),
@@ -494,7 +591,7 @@
             jax.ShapeDtypeStruct(output_map.shape, F32),
             jax.ShapeDtypeStruct(level_table.shape, F32),
         ),
-        in_specs=[vmem, vmem, vmem, vmem, smem, vmem, vmem],
+        in_specs=[hbm, hbm, hbm, hbm, smem, hbm, hbm],
         out_specs=(vmem,) * 6,
         scratch_shapes=[
             pltpu.VMEM(tall, F32),
@@ -538,6 +635,15 @@
             dma((nb,)),
             pltpu.VMEM((heads, 2, LANES), F32),
             pltpu.VMEM((heads, 2, LANES), F32),
+            pltpu.VMEM((2, pairs, 2 * state, LANES), BF16),
+            pltpu.VMEM((2, *unit), BF16),
+            pltpu.VMEM(inputs.shape, BF16),
+            pltpu.VMEM(step_sizes.shape, F32),
+            pltpu.VMEM(input_map.shape, BF16),
+            pltpu.VMEM(output_map.shape, BF16),
+            pltpu.VMEM((1, tokens), jnp.int32),
+            pltpu.VMEM(cotangent.shape, BF16),
+            dma((6,)),
         ],
         compiler_params=pltpu.CompilerParams(
             collective_id=0, has_side_effects=True, vmem_limit_bytes=48 << 20
@@ -546,6 +652,14 @@
         inputs, step_sizes, input_map, output_map, level_table,
         token_class.reshape(1, tokens), cotangent,
     )
+    return pl.pallas_call(
+        write_out,
+        out_shape=tuple(jax.ShapeDtypeStruct(r.shape, r.dtype) for r in results),
+        in_specs=[vmem] * 6,
+        out_specs=(hbm,) * 6,
+        scratch_shapes=[dma((6,))],
+        compiler_params=pltpu.CompilerParams(vmem_limit_bytes=8 << 20),
+    )(*results)
 
 
 def solution(mesh):

time: 49.1 us -> 44.4 us (0.904)
  local copies, waits for them, and re-layouts: 9.68 us -> 5.71 us
  Pallas kernels: 38.4 us -> 37.6 us
    unnamed x20 -> x14, local copies, waits for them, and re-layouts: 9.68 us -> 5.71 us
    pallas_call x1, Pallas kernels: 38.4 us -> 36.6 us  [local(): pl.pallas_call(functools.partial(kernel, dims), out_shape=(jax.ShapeDtype...]
    pallas_call x0 -> x1, Pallas kernels: none -> 0.98 us  [local(): pl.pallas_call(write_out, out_shape=tuple((jax.ShapeDtypeStruct(r.shape,...]
where the time goes in v1:
time: 44.4 us; the launch traced here: 44 us
  Pallas kernels  37.6 us (85%)
  local copies, waits for them, and re-layouts  5.71 us (13%)
  between operations  0.66 us (1%)
    pallas_call x1, Pallas kernels, local(): pl.pallas_call(functools.partial(kernel, dims), out_shape=(jax.ShapeDtype...  36.6 us
    unnamed x14, local copies, waits for them, and re-layouts  5.71 us
    pallas_call x1, Pallas kernels, local(): pl.pallas_call(write_out, out_shape=tuple((jax.ShapeDtypeStruct(r.shape,...  0.98 us

profile of v1, /device:TPU:0, one launch (start us, length us, event | category | flops | bytes accessed | tf_op | source)
XLA Modules:
  0.0 44.0 jit_solution(13643863049312189662)
XLA Ops:
  0.6 0.0 copy-start.6
  0.6 0.7 %copy-done.6 = s32[256]{0:T(256)S(1)} copy-done((s32[256]{0:T(256)S(1)}, s32[256]{0:T(256)}, u32[]{:S(2)}) %copy-start.6) | copy-done | bytes 1048
  1.3 0.0 copy-start
  1.3 1.0 %copy-done = bf16[256,640]{1,0:T(8,128)(2,1)S(1)} copy-done((bf16[256,640]{1,0:T(8,128)(2,1)S(1)}, bf16[256,640]{1,0:T(8,128)(2,1)}, u32[]{:S(2)}) %copy-start) | copy-done | bytes 327704
  2.3 0.0 copy-start.1
  2.3 1.0 %copy-done.1 = bf16[256,640]{1,0:T(8,128)(2,1)S(1)} copy-done((bf16[256,640]{1,0:T(8,128)(2,1)S(1)}, bf16[256,640]{1,0:T(8,128)(2,1)}, u32[]{:S(2)}) %copy-start.1) | copy-done | bytes 327704
  3.3 0.0 copy-start.2
  3.3 0.8 %copy-done.2 = bf16[256,128]{1,0:T(8,128)(2,1)S(1)} copy-done((bf16[256,128]{1,0:T(8,128)(2,1)S(1)}, bf16[256,128]{1,0:T(8,128)(2,1)}, u32[]{:S(2)}) %copy-start.2) | copy-done | bytes 65560
  4.1 0.0 copy-start.3
  4.1 0.8 %copy-done.3 = bf16[256,128]{1,0:T(8,128)(2,1)S(1)} copy-done((bf16[256,128]{1,0:T(8,128)(2,1)S(1)}, bf16[256,128]{1,0:T(8,128)(2,1)}, u32[]{:S(2)}) %copy-start.3) | copy-done | bytes 65560
  4.9 0.0 copy-start.4
  4.9 0.7 %copy-done.4 = f32[10,256]{1,0:T(8,128)S(1)} copy-done((f32[10,256]{1,0:T(8,128)S(1)}, f32[10,256]{1,0:T(8,128)}, u32[]{:S(2)}) %copy-start.4) | copy-done | bytes 10264
  5.7 0.0 copy-start.5
  5.7 0.7 %copy-done.5 = f32[10,2,12]{2,1,0:T(2,128)S(1)} copy-done((f32[10,2,12]{2,1,0:T(2,128)S(1)}, f32[10,2,12]{2,1,0:T(2,128)}, u32[]{:S(2)}) %copy-start.5) | copy-done | bytes 984
  6.4 36.6 %shard_map.118 = (bf16[256,640]{1,0:T(8,128)(2,1)S(1)}, bf16[256,640]{1,0:T(8,128)(2,1)S(1)}, f32[10,256]{1,0:T(8,128)S(1)}, f32[256,128]{1,0:T(8,128)S(1)}, f32...) custom-call(bf16[256,640]{1,0:T(8,128)(2,1)S(1)} %copy-done, f32[10,256]{1,0:T(8,128)S(1)} %copy-done.4, ...), custom_call_target="tpu_custom_call" | custom-call | tf_op jit(solution)/shard_map/pallas_call | solution.py:584
  43.0 1.0 %shard_map.119 = (bf16[256,640]{1,0:T(8,128)(2,1)}, bf16[256,640]{1,0:T(8,128)(2,1)}, f32[10,256]{1,0:T(8,128)}, f32[256,128]{1,0:T(8,128)}, f32[256,128]{1,0:T(8,128)}, /*index=5*/f32[10,2,12]{2,1,0:T(2,128)}) custom-call(bf16[256,640]{1,0:T(8,128)(2,1)S(1)} %get-tuple-element.12.refs_0_, bf16[256,640]{1,0:T(8,128)(2,1)S(1)} %get-tuple-element.13.refs_1_, ...), custom_call_target="tpu_custom_call" | custom-call | tf_op jit(solution)/shard_map/pallas_call | solution.py:655
Async XLA Ops:
  0.6 0.7 %copy-start.6 = (s32[256]{0:T(256)S(1)}, s32[256]{0:T(256)}, u32[]{:S(2)}) copy-start(s32[256]{0:T(256)} %param.12) | copy-start | bytes 3076
  1.3 1.0 %copy-start = (bf16[256,640]{1,0:T(8,128)(2,1)S(1)}, bf16[256,640]{1,0:T(8,128)(2,1)}, u32[]{:S(2)}) copy-start(bf16[256,640]{1,0:T(8,128)(2,1)} %x_hbm.1) | copy-start | bytes 983044
  2.3 1.0 %copy-start.1 = (bf16[256,640]{1,0:T(8,128)(2,1)S(1)}, bf16[256,640]{1,0:T(8,128)(2,1)}, u32[]{:S(2)}) copy-start(bf16[256,640]{1,0:T(8,128)(2,1)} %g_hbm.1) | copy-start | bytes 983044
  3.3 0.8 %copy-start.2 = (bf16[256,128]{1,0:T(8,128)(2,1)S(1)}, bf16[256,128]{1,0:T(8,128)(2,1)}, u32[]{:S(2)}) copy-start(bf16[256,128]{1,0:T(8,128)(2,1)} %bin_hbm.1) | copy-start | bytes 196612
  4.1 0.8 %copy-start.3 = (bf16[256,128]{1,0:T(8,128)(2,1)S(1)}, bf16[256,128]{1,0:T(8,128)(2,1)}, u32[]{:S(2)}) copy-start(bf16[256,128]{1,0:T(8,128)(2,1)} %cout_hbm.1) | copy-start | bytes 196612
  4.9 0.7 %copy-start.4 = (f32[10,256]{1,0:T(8,128)S(1)}, f32[10,256]{1,0:T(8,128)}, u32[]{:S(2)}) copy-start(f32[10,256]{1,0:T(8,128)} %step_hbm.1) | copy-start | bytes 30724
  5.7 0.7 %copy-start.5 = (f32[10,2,12]{2,1,0:T(2,128)S(1)}, f32[10,2,12]{2,1,0:T(2,128)}, u32[]{:S(2)}) copy-start(f32[10,2,12]{2,1,0:T(2,128)} %table_ref.1) | copy-start | bytes 2884

commit v2 on v1

--- a/solution.py
+++ b/solution.py
@@ -32,7 +32,7 @@
     step_hbm,
     bin_hbm,
     cout_hbm,
-    table_ref,
+    table_hbm,
     class_hbm,
     g_hbm,
     out_ref,
@@ -90,6 +90,7 @@
     cout_ref,
     class_ref,
     g_ref,
+    table_ref,
     in_sem,
 ):
     heads, width, tokens, state, levels, nb, n_head, total = dims
@@ -102,8 +103,8 @@
     mine = lax.axis_index("head")
 
     barrier = pltpu.get_barrier_semaphore()
-    for b in range(nb):
-        pl.semaphore_signal(barrier, inc=1, device_id={"seq": device ^ (1 << b)}, device_id_type=MESH)
+    for i in range(1, 1 << nb):
+        pl.semaphore_signal(barrier, inc=1, device_id={"seq": device ^ i}, device_id_type=MESH)
     for i in range(1, n_head):
         pl.semaphore_signal(
             barrier, inc=1, device_id={"head": lax.rem(mine + i, n_head)}, device_id_type=MESH
@@ -119,6 +120,7 @@
                 (step_hbm, step_ref),
                 (x_hbm, x_ref),
                 (g_hbm, g_ref),
+                (table_hbm, table_ref),
             ]
         )
     ]
@@ -323,7 +325,7 @@
         states(p, carry)
         return begin(p, carry)
 
-    pl.semaphore_wait(barrier, nb + n_head - 1)
+    pl.semaphore_wait(barrier, (1 << nb) - 1 + n_head - 1)
     lax.fori_loop(0, pairs, states_begin, 0)
 
     def near(p, carry):
@@ -476,10 +478,10 @@
 
     for i in range(1, n_head):
         part_copy(i).start()
-    def table_copy(b):
+    def table_copy(i):
         return pltpu.make_async_remote_copy(
-            tsend.at[b], trecv.at[b], t_ssem.at[b], t_rsem.at[b],
-            device_id={"seq": device ^ (1 << b)}, device_id_type=MESH,
+            tsend, trecv.at[i], t_ssem.at[i], t_rsem.at[i],
+            device_id={"seq": device ^ i}, device_id_type=MESH,
         )
 
     table_sum = []
@@ -490,29 +492,28 @@
             acc = jnp.where(lane == level, col * (scale_of(level) / math.sqrt(total)), acc)
         table_sum.append(acc)
     for k in range(2):
-        tsend[0, k, :heads, :] = table_sum[k]
-    table_copy(0).start()
+        tsend[k, :heads, :] = table_sum[k]
+        trecv[0, k, :heads, :] = table_sum[k]
+    for i in range(1, 1 << nb):
+        table_copy(i).start()
 
     far_values(pairs - 1)
     for h in range(heads):
         for c in range(2):
             sg_ref[h : h + 1, spans[c]] = sgrow[h, c : c + 1, :]
-    for b in range(nb):
-        table_copy(b).wait_recv()
-        for k in range(2):
-            table_sum[k] = table_sum[k] + trecv[b, k, :heads, :]
-        if b + 1 < nb:
-            for k in range(2):
-                tsend[b + 1, k, :heads, :] = table_sum[k]
-            table_copy(b + 1).start()
-        if b == 0:
-            summed = part_own[mine]
-            for i in range(1, n_head):
-                part_copy(i).wait_recv()
-                summed = summed + part_recv[i].astype(F32)
-            final[mine] = summed.astype(BF16)
-            for i in range(1, n_head):
-                all_copy(i, mine).start()
+    summed = part_own[mine]
+    for i in range(1, n_head):
+        part_copy(i).wait_recv()
+        summed = summed + part_recv[i].astype(F32)
+    final[mine] = summed.astype(BF16)
+    for i in range(1, n_head):
+        all_copy(i, mine).start()
+    for i in range(1, 1 << nb):
+        table_copy(i).wait_recv()
+    for k in range(2):
+        table_sum[k] = trecv[device, k, :heads, :]
+        for owner in range(1, 1 << nb):
+            table_sum[k] = table_sum[k] + trecv[device ^ owner, k, :heads, :]
     for k in range(2):
         tg_ref[:, k, :] = table_sum[k][:, :levels]
     for i in range(1, n_head):
@@ -525,8 +526,9 @@
     for i in range(1, n_head):
         part_copy(i).wait_send()
         all_copy(i, mine).wait_send()
+    for i in range(1, 1 << nb):
+        table_copy(i).wait_send()
     for b in range(nb):
-        table_copy(b).wait_send()
 
         def drain(p, carry, b=b):
             @pl.when(f_sent[b])
@@ -576,11 +578,17 @@
     rows = 2 * tokens // n_head
     vmem = pl.BlockSpec(memory_space=pltpu.VMEM)
     hbm = pl.BlockSpec(memory_space=pltpu.HBM)
-    smem = pl.BlockSpec(memory_space=pltpu.SMEM)
     dma = pltpu.SemaphoreType.DMA
     unit = (pairs, state, LANES)
     tall = (pairs, tokens, LANES)
     padded = -(-heads // 8) * 8
+    placed = [
+        pltpu.with_memory_space_constraint(a, pltpu.HBM)
+        for a in (
+            inputs, step_sizes, input_map, output_map, level_table,
+            token_class.reshape(1, tokens), cotangent,
+        )
+    ]
     results = pl.pallas_call(
         functools.partial(kernel, dims),
         out_shape=(
@@ -591,7 +599,7 @@
             jax.ShapeDtypeStruct(output_map.shape, F32),
             jax.ShapeDtypeStruct(level_table.shape, F32),
         ),
-        in_specs=[hbm, hbm, hbm, hbm, smem, hbm, hbm],
+        in_specs=[hbm] * 7,
         out_specs=(vmem,) * 6,
         scratch_shapes=[
             pltpu.VMEM(tall, F32),
@@ -621,8 +629,8 @@
             pltpu.VMEM((n_head, rows, state), BF16),
             pltpu.VMEM((n_head, rows, state), F32),
             pltpu.VMEM((n_head, rows, state), BF16),
-            pltpu.VMEM((nb, 2, padded, LANES), F32),
-            pltpu.VMEM((nb, 2, padded, LANES), F32),
+            pltpu.VMEM((2, padded, LANES), F32),
+            pltpu.VMEM((n_seq, 2, padded, LANES), F32),
             dma((nb, pairs)),
             dma((nb, pairs)),
             dma((nb, 2, pairs)),
@@ -631,8 +639,8 @@
             dma((n_head,)),
             dma((n_head,)),
             dma((n_head,)),
-            dma((nb,)),
-            dma((nb,)),
+            dma((n_seq,)),
+            dma((n_seq,)),
             pltpu.VMEM((heads, 2, LANES), F32),
             pltpu.VMEM((heads, 2, LANES), F32),
             pltpu.VMEM((2, pairs, 2 * state, LANES), BF16),
@@ -643,15 +651,13 @@
             pltpu.VMEM(output_map.shape, BF16),
             pltpu.VMEM((1, tokens), jnp.int32),
             pltpu.VMEM(cotangent.shape, BF16),
-            dma((6,)),
+            pltpu.SMEM(level_table.shape, F32),
+            dma((7,)),
         ],
         compiler_params=pltpu.CompilerParams(
             collective_id=0, has_side_effects=True, vmem_limit_bytes=48 << 20
         ),
-    )(
-        inputs, step_sizes, input_map, output_map, level_table,
-        token_class.reshape(1, tokens), cotangent,
-    )
+    )(*placed)
     return pl.pallas_call(
         write_out,
         out_shape=tuple(jax.ShapeDtypeStruct(r.shape, r.dtype) for r in results),

time: 44.4 us -> 34.6 us (0.78)
  local copies, waits for them, and re-layouts: 5.71 us -> 0 us
  Pallas kernels: 37.6 us -> 33.4 us
    unnamed x14 -> x0, local copies, waits for them, and re-layouts: 5.71 us -> none
    pallas_call x1, Pallas kernels: 36.6 us -> 32.4 us  [local(): pl.pallas_call(functools.partial(kernel, dims), out_shape=(jax.ShapeDtype...]
where the time goes in v2:
time: 34.6 us; the launch traced here: 34 us
  Pallas kernels  33.4 us (97%)
  between operations  0.64 us (2%)
    pallas_call x1, Pallas kernels, local(): pl.pallas_call(functools.partial(kernel, dims), out_shape=(jax.ShapeDtype...  32.4 us
    pallas_call x1, Pallas kernels, local(): pl.pallas_call(write_out, out_shape=tuple((jax.ShapeDtypeStruct(r.shape,...  0.98 us

profile of v2, /device:TPU:0, one launch (start us, length us, event | category | flops | bytes accessed | tf_op | source)
XLA Modules:
  0.0 34.0 jit_solution(17537420681767570923)
XLA Ops:
  0.6 32.4 %shard_map.118 = (bf16[256,640]{1,0:T(8,128)(2,1)S(1)}, bf16[256,640]{1,0:T(8,128)(2,1)S(1)}, f32[10,256]{1,0:T(8,128)S(1)}, f32[256,128]{1,0:T(8,128)S(1)}, f32...) custom-call(bf16[256,640]{1,0:T(8,128)(2,1)} %x_hbm.1, f32[10,256]{1,0:T(8,128)} %step_hbm.1, bf16[256,128]{1,0:T(8,128)(2,1)} %bin_hbm.1, ...), custom_call_target="tpu_custom_call" | custom-call | tf_op jit(solution)/shard_map/pallas_call | solution.py:592
  33.0 1.0 %shard_map.119 = (bf16[256,640]{1,0:T(8,128)(2,1)}, bf16[256,640]{1,0:T(8,128)(2,1)}, f32[10,256]{1,0:T(8,128)}, f32[256,128]{1,0:T(8,128)}, f32[256,128]{1,0:T(8,128)}, /*index=5*/f32[10,2,12]{2,1,0:T(2,128)}) custom-call(bf16[256,640]{1,0:T(8,128)(2,1)S(1)} %get-tuple-element.12.refs_0_, bf16[256,640]{1,0:T(8,128)(2,1)S(1)} %get-tuple-element.13.refs_1_, ...), custom_call_target="tpu_custom_call" | custom-call | tf_op jit(solution)/shard_map/pallas_call | solution.py:661

commit v3 on v2

--- a/solution.py
+++ b/solution.py
@@ -142,7 +142,7 @@
     def cols(p):
         return pl.ds(pl.multiple_of(p * LANES, LANES), LANES)
 
-    for load in loads:
+    for load in loads[:4]:
         load.wait()
     row = class_ref[...].astype(F32)
     clsb[...] = dot(
@@ -325,6 +325,8 @@
         states(p, carry)
         return begin(p, carry)
 
+    for load in loads[4:]:
+        load.wait()
     pl.semaphore_wait(barrier, (1 << nb) - 1 + n_head - 1)
     lax.fori_loop(0, pairs, states_begin, 0)
 

time: 34.6 us -> 34.4 us (level); the launches traced: 34 us -> 34.2 us
  no operation moved by 1% of the time
where the time goes in v3:
time: 34.4 us; the launch traced here: 34.2 us
  Pallas kernels  33.6 us (98%)
  between operations  0.64 us (2%)
    pallas_call x1, Pallas kernels, local(): pl.pallas_call(functools.partial(kernel, dims), out_shape=(jax.ShapeDtype...  32.6 us
    pallas_call x1, Pallas kernels, local(): pl.pallas_call(write_out, out_shape=tuple((jax.ShapeDtypeStruct(r.shape,...  0.98 us

profile of v3, /device:TPU:0, one launch (start us, length us, event | category | flops | bytes accessed | tf_op | source)
XLA Modules:
  0.0 34.2 jit_solution(17266200731721228757)
XLA Ops:
  0.6 32.6 %shard_map.118 = (bf16[256,640]{1,0:T(8,128)(2,1)S(1)}, bf16[256,640]{1,0:T(8,128)(2,1)S(1)}, f32[10,256]{1,0:T(8,128)S(1)}, f32[256,128]{1,0:T(8,128)S(1)}, f32...) custom-call(bf16[256,640]{1,0:T(8,128)(2,1)} %x_hbm.1, f32[10,256]{1,0:T(8,128)} %step_hbm.1, bf16[256,128]{1,0:T(8,128)(2,1)} %bin_hbm.1, ...), custom_call_target="tpu_custom_call" | custom-call | tf_op jit(solution)/shard_map/pallas_call | solution.py:594
  33.2 1.0 %shard_map.119 = (bf16[256,640]{1,0:T(8,128)(2,1)}, bf16[256,640]{1,0:T(8,128)(2,1)}, f32[10,256]{1,0:T(8,128)}, f32[256,128]{1,0:T(8,128)}, f32[256,128]{1,0:T(8,128)}, /*index=5*/f32[10,2,12]{2,1,0:T(2,128)}) custom-call(bf16[256,640]{1,0:T(8,128)(2,1)S(1)} %get-tuple-element.12.refs_0_, bf16[256,640]{1,0:T(8,128)(2,1)S(1)} %get-tuple-element.13.refs_1_, ...), custom_call_target="tpu_custom_call" | custom-call | tf_op jit(solution)/shard_map/pallas_call | solution.py:663
